TPU v7x, 32 devices: a whole 2x2x4 slice. The times are simulated.
32 devices in a mesh: dp: 4 (over z), seq: 8 (over y, x, core).
Axes of the slice: x: 2, y: 2, z: 4, core: 2. Of those that a mesh axis runs over, the one named last changes fastest.
Arguments:
- slide_tiles: bfloat16 [64, 256, 384], P(('dp', 'seq')), parts along dimension 0, may hold values from -6 to 6
- norm_gain: float32 [2, 384], replicated, may hold values from 0.1 to 1.9
- in_weight: bfloat16 [2, 384, 1536], replicated, may hold values from -0.3125 to 0.3125
- state_weight: bfloat16 [2, 384, 44], replicated, may hold values from -0.3125 to 0.3125
- conv_weight: float32 [2, 4, 800], replicated, may hold values from -2.5 to 2.5
- conv_bias: float32 [2, 800], replicated, may hold values from -0.5 to 0.5
- step_bias: float32 [2, 12], replicated, may hold values from -5 to -3
- decay_log: float32 [2, 12], replicated, may hold values from -8.5 to 1
- skip_gain: float32 [2, 12], replicated, may hold values from 0.5 to 1.5
- out_gain: float32 [2, 768], replicated, may hold values from 0.1 to 1.9
- out_weight: bfloat16 [2, 768, 384], replicated, may hold values from -0.21875 to 0.21875
Outputs:
- tile_out: bfloat16 [64, 256, 384], P(('dp', 'seq')), parts along dimension 0
There are 4 independent parts, one for each index of `dp`. A program takes and returns all parts, laid end to end along the dimension named above; an argument that names none is the same for every part. Nothing has to cross between parts.
All inputs are finite; a program needn't handle non-finite values.
Results may differ from a plain program's by a relative error of at most 0.014.
Values may be sent and summed in bfloat16 or wider, within the bound.
A program may use at most 64 MiB of HBM per device.

v0:
```python
import jax
import jax.numpy as jnp
from jax import lax
from jax.sharding import PartitionSpec as P

HEADS = 12
HEADDIM = 64
STATE = 16
GROUP = 256
epsilon = 1e-05


def entering_2(x, axis, join, neutral):
    place = lax.axis_index(axis)
    gathered = jax.tree.map(
        lambda a, kind: lax.all_gather(a.astype(kind), axis), x, (jnp.bfloat16, jnp.bfloat16)
    )
    state = jax.tree.map(lambda a, e: jnp.zeros_like(a) + jnp.asarray(e, a.dtype), x, neutral)

    def one(step, state):
        return join(
            state,
            jax.tree.map(
                lambda a, own: lax.dynamic_index_in_dim(a, step, 0, False).astype(own.dtype),
                gathered,
                x,
            ),
        )

    return lax.fori_loop(0, place, one, state)


def passed_along(value, axis, steps):
    count = lax.axis_size(axis)
    first, last = (max(0, -steps), min(count, count - steps))
    return lax.ppermute(value, axis, [(source, source + steps) for source in range(first, last)])


def rms_scaled(values, scale_gain):
    values = values.astype(jnp.float32)
    return (
        values * lax.rsqrt(jnp.mean(values * values, axis=-1, keepdims=True) + epsilon) * scale_gain
    )


def group_terms(group_in):
    group_x, group_b, group_c, group_step, group_rate = group_in
    cumulative = jnp.cumsum(group_rate, axis=0)
    positions = jnp.arange(group_x.shape[0])
    lower_mask = positions[:, None] >= positions[None, :]
    cum_heads = cumulative.T
    differences = cum_heads[:, :, None] - cum_heads[:, None, :]
    decay_mask = jnp.exp(jnp.where(lower_mask[None], differences, -jnp.inf))
    scores = jnp.dot(group_c, group_b.T, preferred_element_type=jnp.float32)
    weights = (scores[None] * decay_mask * group_step.T[:, None, :]).astype(jnp.bfloat16)
    intra_out = jnp.einsum("hts,shp->thp", weights, group_x, preferred_element_type=jnp.float32)
    tail_weight = jnp.exp(cumulative[-1][None, :] - cumulative) * group_step
    weighted_x = (group_x.astype(jnp.float32) * tail_weight[:, :, None]).astype(jnp.bfloat16)
    local_state = jnp.einsum("shp,sn->hpn", weighted_x, group_b, preferred_element_type=jnp.float32)
    return (intra_out, local_state, cumulative)


def link_states(earlier, latter):
    return (earlier[0] + latter[0], jnp.exp(latter[0])[:, None, None] * earlier[1] + latter[1])


def incoming_state(whole_decay, final_state):
    identity = (jnp.zeros_like(whole_decay), jnp.zeros_like(final_state))
    passed = entering_2((whole_decay, final_state), "seq", link_states, identity)
    return passed[1]


def advance(carry_state, group_item):
    group_total, local_state = group_item
    return (jnp.exp(group_total)[:, None, None] * carry_state + local_state, carry_state)


def mixer(
    sequence,
    layer,
    norm_gain,
    in_weight,
    state_weight,
    conv_weight,
    conv_bias,
    step_bias,
    decay_log,
    skip_gain,
    out_gain,
):
    length = sequence.shape[0]
    inner_width = in_weight.shape[2] // 2
    normed = rms_scaled(sequence, norm_gain[layer]).astype(jnp.bfloat16)
    gate_x = jnp.dot(normed, in_weight[layer], preferred_element_type=jnp.float32).astype(
        jnp.bfloat16
    )
    state_proj = jnp.dot(normed, state_weight[layer], preferred_element_type=jnp.float32).astype(
        jnp.bfloat16
    )
    x_part = gate_x[:, inner_width:]
    bc_part = state_proj[:, : 2 * STATE]
    margin = conv_weight.shape[1] - 1
    edge_rows = passed_along((x_part[length - margin :], bc_part[length - margin :]), "seq", 1)
    x_padded = jnp.concatenate([edge_rows[0], x_part], axis=0)
    bc_padded = jnp.concatenate([edge_rows[1], bc_part], axis=0)
    taps = conv_weight[layer]
    conv_x = jnp.zeros((length, inner_width), jnp.float32) + conv_bias[layer][None, :inner_width]
    conv_bc = jnp.zeros((length, 2 * STATE), jnp.float32) + conv_bias[layer][None, inner_width:]
    for offset in range(margin + 1):
        conv_x = conv_x + taps[offset][None, :inner_width] * x_padded[
            offset : offset + length
        ].astype(jnp.float32)
        conv_bc = conv_bc + taps[offset][None, inner_width:] * bc_padded[
            offset : offset + length
        ].astype(jnp.float32)
    x_conv = jax.nn.silu(conv_x).astype(jnp.bfloat16)
    bc_conv = jax.nn.silu(conv_bc).astype(jnp.bfloat16)
    step_size = jax.nn.softplus(
        state_proj[:, 2 * STATE :].astype(jnp.float32) + step_bias[layer][None, :]
    )
    log_rates = -step_size * jnp.exp(decay_log[layer])[None, :]
    group_count = length // GROUP
    group_x = x_conv.reshape(group_count, GROUP, HEADS, HEADDIM)
    group_c = bc_conv[:, STATE:].reshape(group_count, GROUP, STATE)
    inputs = (
        group_x,
        bc_conv[:, :STATE].reshape(group_count, GROUP, STATE),
        group_c,
        step_size.reshape(group_count, GROUP, HEADS),
        log_rates.reshape(group_count, GROUP, HEADS),
    )
    intra_out, local_states, cumulative = lax.map(group_terms, inputs)
    totals = cumulative[:, -1, :]
    final_state, entering = lax.scan(
        advance, jnp.zeros((HEADS, HEADDIM, STATE), jnp.float32), (totals, local_states)
    )
    arriving = incoming_state(jnp.sum(totals, axis=0), final_state)
    before = jnp.cumsum(totals, axis=0) - totals
    start_states = entering + jnp.exp(before)[:, :, None, None] * arriving[None]
    inter_out = jnp.exp(cumulative)[..., None] * jnp.einsum(
        "ctn,chpn->cthp", group_c.astype(jnp.float32), start_states, precision=lax.Precision.HIGHEST
    )
    y_total = (
        intra_out + inter_out + skip_gain[layer][None, None, :, None] * group_x.astype(jnp.float32)
    )
    gated = y_total.reshape(length, inner_width) * jax.nn.silu(
        gate_x[:, :inner_width].astype(jnp.float32)
    )
    return rms_scaled(gated, out_gain[layer]).astype(jnp.bfloat16)


def on_device(
    slide_tiles,
    norm_gain,
    in_weight,
    state_weight,
    conv_weight,
    conv_bias,
    step_bias,
    decay_log,
    skip_gain,
    out_gain,
    out_weight,
):
    row_count, col_count, feature_count = slide_tiles.shape
    params = (
        norm_gain,
        in_weight,
        state_weight,
        conv_weight,
        conv_bias,
        step_bias,
        decay_log,
        skip_gain,
        out_gain,
    )
    flipped = slide_tiles[:, ::-1, :]
    columns = lax.all_to_all(flipped, "seq", split_axis=1, concat_axis=0, tiled=True)
    full_rows, block_cols = (columns.shape[0], columns.shape[1])
    first_order = jnp.transpose(columns[::-1], (1, 0, 2)).reshape(
        full_rows * block_cols, feature_count
    )
    mixed_out = mixer(first_order, 0, *params)
    layer_out = (
        first_order.astype(jnp.float32)
        + jnp.dot(mixed_out, out_weight[0], preferred_element_type=jnp.float32)
    ).astype(jnp.bfloat16)
    row_grid = jnp.transpose(layer_out.reshape(block_cols, full_rows, feature_count), (1, 0, 2))[
        ::-1
    ]
    returned = lax.all_to_all(row_grid, "seq", split_axis=0, concat_axis=1, tiled=True)
    second = returned[:, ::-1, :].reshape(row_count * col_count, feature_count)
    mixed_out = mixer(second, 1, *params)
    result = (
        second.astype(jnp.float32)
        + jnp.dot(mixed_out, out_weight[1], preferred_element_type=jnp.float32)
    ).astype(jnp.bfloat16)
    return result.reshape(row_count, col_count, feature_count)


def solution(mesh):
    placed = (P(("dp", "seq"), None, None), P(), P(), P(), P(), P(), P(), P(), P(), P(), P())
    return jax.shard_map(
        on_device,
        mesh=mesh,
        in_specs=placed,
        out_specs=P(("dp", "seq"), None, None),
        check_vma=False,
    )
```

profile of v0, /device:TPU:0, one launch (start us, length us, event | category | flops | bytes accessed | tf_op | source)
XLA Modules:
  0.0 138.6 jit_solution(18102543792137817311)
XLA Ops:
  0.1 1.5 %copy.98 = bf16[2,256,384]{2,0,1:T(2,128)(2,1)S(1)} copy(bf16[2,256,384]{2,1,0:T(8,128)(2,1)} %param.23) | data formatting | bytes 786432 | tf_op args[0]
  1.5 1.0 rev.12
  2.5 5.2 %all-to-all-start = ((bf16[2,256,384]{2,0,1:T(2,128)(2,1)}), bf16[2,256,384]{2,0,1:T(2,128)(2,1)S(1)}, u32[]{:S(2)}, u32[]{:S(2)}) async-start(bf16[2,256,384]{2,0,1:T(2,128)(2,1)} %rev.12), calls=%async_computation | async-start | bytes 786432 | tf_op jit(solution)/shard_map/all_to_all | solution.py:178
  8.3 0.6 slice_reduce_fusion.13
  8.9 0.6 slice_reduce_fusion.20
  9.5 0.6 slice_bitcast_fusion.5
  10.1 0.5 slice_bitcast_fusion
  10.6 0.6 slice_reduce_fusion.8
  11.2 0.6 exponential_bitcast_fusion.2
  11.8 0.6 dynamic-slice
  13.0 0.6 slice_reduce_fusion.12
  13.6 0.7 fusion.105
  14.3 1.7 %all-to-all-done = bf16[2,256,384]{2,0,1:T(2,128)(2,1)S(1)} async-done(((bf16[2,256,384]{2,0,1:T(2,128)(2,1)}), bf16[2,256,384]{2,0,1:T(2,128)(2,1)S(1)}, u32[]{:S(2)}, u32[]{:S(2)}) %all-to-all-start) | async-done | bytes 393248 | tf_op jit(solution)/shard_map/all_to_all | solution.py:178
  17.5 2.3 %convolution_convert_fusion.1 = bf16[512,1536]{1,0:T(8,128)(2,1)S(1)} fusion(bf16[512,384]{1,0:T(8,128)(2,1)S(1)} %bitcast.348, bf16[2,384,1536]{2,1,0:T(8,128)(2,1)} %param.25), kind=kOutput, calls=%fused_computation.95 | convolution fusion | flops 604766208 | bytes 3145728 | tf_op jit(solution)/shard_map/dot_general | solution.py:94
  19.8 1.0 convert_element_type.292
  21.1 1.3 collective-permute-start.1
  22.4 3.2 %collective-permute-start = (bf16[3,768]{1,0:T(4,128)(2,1)S(1)}, bf16[3,768]{1,0:T(4,128)(2,1)S(1)}, u32[]{:S(2)}, u32[]{:S(2)}) collective-permute-start(bf16[3,768]{1,0:T(4,128)(2,1)S(1)} %slice.368), channel_id=1, source_target_pairs={{0,1},{1,2},{2,3},{3,4},{4,5},{5,6},{6,7},{8,9},{9,10},{10,11},{11... | collective-permute-start | bytes 13832 | tf_op jit(solution)/shard_map/ppermute | solution.py:36
  26.0 0.6 reshape.377
  26.6 1.1 multiply_convert_fusion.17
  28.5 0.6 broadcast.140.clone
  29.1 8.0 %while.78 = (s32[]{:T(128)}, f32[2,256,12,64]{1,3,2,0:T(8,128)S(1)}, f32[2,12,64,16]{2,3,1,0:T(8,128)S(1)}, f32[2,256,12]{1,2,0:T(8,128)}, bf16[2,256,12,64]{1,3...) while((s32[]{:T(128)}, ...), condition=%wide.region_4.5_spmd, body=%wide.region_1.4_spmd.sunk | while | flops 114038824 | bytes 2966549 | solution.py:132
  29.1 0.6 copy-done.9
  29.7 0.6 reduce-window.24
  30.9 1.0 fusion.138
  32.4 0.6 bitcast_dynamic-update-slice_fusion.8
  33.1 0.6 copy-done.9
  33.7 0.6 reduce-window.24
  34.9 1.0 fusion.138
  36.4 0.6 bitcast_dynamic-update-slice_fusion.8
  37.0 1.0 slice_reduce_fusion.6
  38.0 0.8 exp.113
  39.2 10.9 %all-gather.1 = bf16[96,64,16]{1,2,0:T(8,128)(2,1)S(1)} all-gather(bf16[12,64,16]{1,2,0:T(8,128)(2,1)S(1)} %convert_element_type.257), channel_id=3, replica_groups=mesh['dp'=4,'seq'=8] {'seq'}, dimensions={0}, use_global_device_ids=true | all-gather | bytes 221184 | tf_op jit(solution)/shard_map/all_gather | solution.py:16
  50.3 13.2 %all-reduce = bf16[96]{0:T(256)(128)(2,1)S(1)} all-reduce(bf16[96]{0:T(256)(128)(2,1)S(1)} %dynamic-update-slice), channel_id=2, replica_groups=mesh['dp'=4,'seq'=8] {'seq'}, use_global_device_ids=true, to_apply=%add | all-reduce | flops 96 | bytes 384
  63.9 1.3 multiply_add_fusion.1
  65.2 1.2 copy.109
  67.1 1.9 %multiply_reduce_fusion.1 = f32[512]{0:T(512)S(1)} fusion(f32[512,768]{1,0:T(8,128)S(1)} %copy.110, bf16[512,1536]{1,0:T(8,128)(2,1)} %copy-done.4), kind=kLoop, calls=%fused_computation.113 | loop fusion | flops 3145216 | bytes 2361344 | tf_op jit(solution)/shard_map/reduce_sum | solution.py:42
  68.9 1.9 %fusion.68 = bf16[512,384]{1,0:T(8,128)(2,1)S(1)} fusion(f32[512,384]{1,0:T(8,128)S(1)} %bitcast.351, f32[768]{0:T(1024)S(1)} %copy-done.25, f32[512]{0:T(512)S(1)} %add_rsqrt_fusion.3, bf16[2,768,384]{2,1,0:T(8,128)(2,1)} %param.33, f32[512,768]{1,0:T(8,128)S(1)} %copy.110, bf16[512,1536]{1,0:T(8,128)(2,1)S(1)} %copy-done.5), kind=kOutput, calls=%fused_computation.118 | convolution fusion | flops 305922048 | bytes 4134912 | tf_op jit(solution)/shard_map/dot_general | solution.py:186
  70.9 0.8 rev.14
  71.7 3.6 %all-to-all-start.1 = ((bf16[16,32,384]{2,1,0:T(8,128)(2,1)}), bf16[16,32,384]{2,1,0:T(8,128)(2,1)S(1)}, u32[]{:S(2)}, u32[]{:S(2)}) async-start(bf16[16,32,384]{2,1,0:T(8,128)(2,1)} %rev.14), calls=%async_computation.1 | async-start | bytes 786432 | tf_op jit(solution)/shard_map/all_to_all | solution.py:191
  75.3 8.2 %all-to-all-done.1 = bf16[16,32,384]{2,1,0:T(8,128)(2,1)S(1)} async-done(((bf16[16,32,384]{2,1,0:T(8,128)(2,1)}), bf16[16,32,384]{2,1,0:T(8,128)(2,1)S(1)}, u32[]{:S(2)}, u32[]{:S(2)}) %all-to-all-start.1) | async-done | bytes 393248 | tf_op jit(solution)/shard_map/all_to_all | solution.py:191
  84.8 2.3 %convolution_convert_fusion = bf16[512,1536]{1,0:T(8,128)(2,1)S(1)} fusion(bf16[512,384]{1,0:T(8,128)(2,1)S(1)} %bitcast.346, bf16[2,384,1536]{2,1,0:T(8,128)(2,1)} %param.25), kind=kOutput, calls=%fused_computation.94 | convolution fusion | flops 604766208 | bytes 3145728 | tf_op jit(solution)/shard_map/dot_general | solution.py:94
  87.2 1.0 copy-done.2
  88.2 1.3 collective-permute-start.3
  89.5 3.2 %collective-permute-start.2 = (bf16[3,768]{1,0:T(4,128)(2,1)S(1)}, bf16[3,768]{1,0:T(4,128)(2,1)S(1)}, u32[]{:S(2)}, u32[]{:S(2)}) collective-permute-start(bf16[3,768]{1,0:T(4,128)(2,1)S(1)} %slice.384), channel_id=1, source_target_pairs={{0,1},{1,2},{2,3},{3,4},{4,5},{5,6},{6,7},{8,9},{9,10},{10,11},{11... | collective-permute-start | bytes 13832 | tf_op jit(solution)/shard_map/ppermute | solution.py:36
  93.1 0.6 reshape.384
  93.7 1.1 multiply_convert_fusion.15
  95.6 0.6 broadcast.140
  96.2 7.9 %while.80 = (s32[]{:T(128)}, f32[2,256,12,64]{1,3,2,0:T(8,128)S(1)}, f32[2,12,64,16]{2,3,1,0:T(8,128)S(1)}, f32[2,256,12]{1,2,0:T(8,128)}, bf16[2,256,12,64]{1,3...) while((s32[]{:T(128)}, ...), condition=%wide.region_16.17_spmd, body=%wide.region_13.16_spmd.sunk | while | flops 114038824 | bytes 2966549 | solution.py:132
  96.3 0.6 copy-done.7
  96.8 0.6 reduce-window.26
  98.0 1.0 fusion.147
  99.6 0.6 bitcast_dynamic-update-slice_fusion.9
  100.2 0.6 copy-done.7
  100.8 0.6 reduce-window.26
  102.0 1.0 fusion.147
  103.5 0.6 bitcast_dynamic-update-slice_fusion.9
  104.1 1.0 slice_reduce_fusion.4
  105.1 0.8 exp.120
  106.3 10.8 %all-gather.3 = bf16[96,64,16]{1,2,0:T(8,128)(2,1)S(1)} all-gather(bf16[12,64,16]{1,2,0:T(8,128)(2,1)S(1)} %convert_element_type.282), channel_id=5, replica_groups=mesh['dp'=4,'seq'=8] {'seq'}, dimensions={0}, use_global_device_ids=true | all-gather | bytes 221184 | tf_op jit(solution)/shard_map/all_gather | solution.py:16
  117.3 13.2 %all-reduce.1 = bf16[96]{0:T(256)(128)(2,1)S(1)} all-reduce(bf16[96]{0:T(256)(128)(2,1)S(1)} %dynamic-update-slice.1), channel_id=4, replica_groups=mesh['dp'=4,'seq'=8] {'seq'}, use_global_device_ids=true, to_apply=%add.1 | all-reduce | flops 96 | bytes 384
  130.9 1.3 multiply_add_fusion
  132.2 1.2 copy.122
  134.1 1.8 %multiply_reduce_fusion = f32[512]{0:T(512)S(1)} fusion(f32[512,768]{1,0:T(8,128)S(1)} %copy.123, bf16[512,1536]{1,0:T(8,128)(2,1)} %copy-done.2), kind=kLoop, calls=%fused_computation.109 | loop fusion | flops 3145216 | bytes 2361344 | tf_op jit(solution)/shard_map/reduce_sum | solution.py:42
  136.0 2.6 %fusion.69 = bf16[512,384]{1,0:T(8,128)(2,1)} fusion(f32[768]{0:T(1024)S(1)} %copy-done.24, f32[512]{0:T(512)S(1)} %add_rsqrt_fusion.1, bf16[2,768,384]{2,1,0:T(8,128)(2,1)} %param.33, f32[512,768]{1,0:T(8,128)S(1)} %copy.123, bf16[512,1536]{1,0:T(8,128)(2,1)S(1)} %copy-done.3, bf16[512,384]{1,0:T(8,128)(2,1)S(1)} %bitcast.336), kind=kOutput, calls=%fused_computation.119 | convolution fusion | flops 306118656 | bytes 3741696 | tf_op jit(solution)/shard_map/dot_general | solution.py:196
  (241 shorter events, 13.7 us)
Async XLA Ops:
  0.0 11.8 %copy-start.39 = (u32[32]{0:T(128)S(1)}, u32[32]{0:T(128)}, u32[]{:S(2)}) copy-start(u32[32]{0:T(128)} %constant.128) | copy-start | bytes 388
  0.0 7.7 %copy-start.22 = (f32[2,800]{1,0:T(2,128)S(1)}, f32[2,800]{1,0:T(2,128)}, u32[]{:S(2)}) copy-start(f32[2,800]{1,0:T(2,128)} %param.28) | copy-start | bytes 19204
  0.0 8.9 %copy-start.26 = (f32[2,384]{1,0:T(2,128)S(1)}, f32[2,384]{1,0:T(2,128)}, u32[]{:S(2)}) copy-start(f32[2,384]{1,0:T(2,128)} %param.24) | copy-start | bytes 9220
  0.0 9.5 %copy-start.15 = (f32[2,4,800]{2,1,0:T(4,128)S(1)}, f32[2,4,800]{2,1,0:T(4,128)}, u32[]{:S(2)}) copy-start(f32[2,4,800]{2,1,0:T(4,128)} %param.27) | copy-start | bytes 76804
  0.0 10.1 %copy-start.36 = (f32[2,12]{1,0:T(2,128)S(1)}, f32[2,12]{1,0:T(2,128)}, u32[]{:S(2)}) copy-start(f32[2,12]{1,0:T(2,128)} %param.31) | copy-start | bytes 292
  0.0 10.6 %copy-start.23 = (f32[2,768]{1,0:T(2,128)S(1)}, f32[2,768]{1,0:T(2,128)}, u32[]{:S(2)}) copy-start(f32[2,768]{1,0:T(2,128)} %param.32) | copy-start | bytes 18436
  0.0 11.2 %copy-start.38 = (f32[2,12]{1,0:T(2,128)S(1)}, f32[2,12]{1,0:T(2,128)}, u32[]{:S(2)}) copy-start(f32[2,12]{1,0:T(2,128)} %param.29) | copy-start | bytes 292
  0.0 11.2 %copy-start.37 = (f32[2,12]{1,0:T(2,128)S(1)}, f32[2,12]{1,0:T(2,128)}, u32[]{:S(2)}) copy-start(f32[2,12]{1,0:T(2,128)} %param.30) | copy-start | bytes 292
  0.0 13.6 %copy-start.11 = (bf16[2,384,44]{1,0,2:T(2,128)(2,1)S(1)}, bf16[2,384,44]{1,0,2:T(2,128)(2,1)}, u32[]{:S(2)}) copy-start(bf16[2,384,44]{1,0,2:T(2,128)(2,1)} %param.26) | copy-start | bytes 202756
  2.5 13.5 %all-to-all-start = ((bf16[2,256,384]{2,0,1:T(2,128)(2,1)}), bf16[2,256,384]{2,0,1:T(2,128)(2,1)S(1)}, u32[]{:S(2)}, u32[]{:S(2)}) async-start(bf16[2,256,384]{2,0,1:T(2,128)(2,1)} %rev.12), calls=%async_computation | async-start | bytes 786432 | tf_op jit(solution)/shard_map/all_to_all | solution.py:178
  19.7 1.4 %copy-start.4 = (bf16[512,1536]{1,0:T(8,128)(2,1)}, bf16[512,1536]{1,0:T(8,128)(2,1)S(1)}, u32[]{:S(2)}) copy-start(bf16[512,1536]{1,0:T(8,128)(2,1)S(1)} %convolution_convert_fusion.1) | copy-start | bytes 4718596
  21.1 4.6 %collective-permute-start.1 = (bf16[3,32]{0,1:T(8,128)(2,1)S(1)}, bf16[3,32]{0,1:T(8,128)(2,1)S(1)}, u32[]{:S(2)}, u32[]{:S(2)}) collective-permute-start(bf16[3,32]{0,1:T(8,128)(2,1)S(1)} %slice.374), channel_id=1, source_target_pairs={{0,1},{1,2},{2,3},{3,4},{4,5},{5,6},{6,7},{8,9},{9,10},{10,11},{11... | collective-permute-start | bytes 584 | tf_op jit(solution)/shard_map/ppermute | solution.py:36
  22.4 4.2 %collective-permute-start = (bf16[3,768]{1,0:T(4,128)(2,1)S(1)}, bf16[3,768]{1,0:T(4,128)(2,1)S(1)}, u32[]{:S(2)}, u32[]{:S(2)}) collective-permute-start(bf16[3,768]{1,0:T(4,128)(2,1)S(1)} %slice.368), channel_id=1, source_target_pairs={{0,1},{1,2},{2,3},{3,4},{4,5},{5,6},{6,7},{8,9},{9,10},{10,11},{11... | collective-permute-start | bytes 13832 | tf_op jit(solution)/shard_map/ppermute | solution.py:36
  29.1 0.6 copy-start.9
  30.9 2.2 %copy-start.10 = (f32[2,256,12]{1,0,2:T(2,128)S(1)}, f32[2,256,12]{1,0,2:T(2,128)}, u32[]{:S(2)}) copy-start(f32[2,256,12]{1,0,2:T(2,128)} %copy-done.9) | copy-start | bytes 73732 | tf_op jit(solution)/shard_map/while
  33.0 0.6 copy-start.9
  34.9 2.2 %copy-start.10 = (f32[2,256,12]{1,0,2:T(2,128)S(1)}, f32[2,256,12]{1,0,2:T(2,128)}, u32[]{:S(2)}) copy-start(f32[2,256,12]{1,0,2:T(2,128)} %copy-done.9) | copy-start | bytes 73732 | tf_op jit(solution)/shard_map/while
  39.2 24.7 %copy-start.14 = (bf16[2,256,16]{1,0,2:T(2,128)(2,1)S(1)}, bf16[2,256,16]{1,0,2:T(2,128)(2,1)}, u32[]{:S(2)}) copy-start(bf16[2,256,16]{1,0,2:T(2,128)(2,1)} %reshape.377) | copy-start | bytes 49156
  39.2 24.7 %copy-start.33 = (f32[12]{0:T(128)S(1)}, f32[12]{0:T(128)}, u32[]{:S(2)}) copy-start(f32[12]{0:T(128)} %get-tuple-element.486) | copy-start | bytes 148
  67.0 1.9 %copy-start.5 = (bf16[512,1536]{1,0:T(8,128)(2,1)S(1)}, bf16[512,1536]{1,0:T(8,128)(2,1)}, u32[]{:S(2)}) copy-start(bf16[512,1536]{1,0:T(8,128)(2,1)} %copy-done.4) | copy-start | bytes 4718596
  67.0 1.9 %copy-start.6 = (f32[16,32,384]{2,0,1:T(8,128)S(1)}, f32[16,32,384]{2,0,1:T(8,128)}, u32[]{:S(2)}) copy-start(f32[16,32,384]{2,0,1:T(8,128)} %convert_element_type.292) | copy-start | bytes 2359300
  67.0 1.9 %copy-start.25 = (f32[768]{0:T(1024)S(1)}, f32[768]{0:T(1024)}, u32[]{:S(2)}) copy-start(f32[768]{0:T(1024)} %get-tuple-element.382) | copy-start | bytes 9220
  71.7 12.6 %copy-start.21 = (f32[384]{0:T(512)S(1)}, f32[384]{0:T(512)}, u32[]{:S(2)}) copy-start(f32[384]{0:T(512)} %get-tuple-element.383) | copy-start | bytes 4612
  71.7 11.8 %all-to-all-start.1 = ((bf16[16,32,384]{2,1,0:T(8,128)(2,1)}), bf16[16,32,384]{2,1,0:T(8,128)(2,1)S(1)}, u32[]{:S(2)}, u32[]{:S(2)}) async-start(bf16[16,32,384]{2,1,0:T(8,128)(2,1)} %rev.14), calls=%async_computation.1 | async-start | bytes 786432 | tf_op jit(solution)/shard_map/all_to_all | solution.py:191
  75.3 9.2 %copy-start.12 = (bf16[1,384,44]{1,0,2:T(2,128)(2,1)S(1)}, bf16[1,384,44]{1,0,2:T(2,128)(2,1)}, u32[]{:S(2)}) copy-start(bf16[1,384,44]{1,0,2:T(2,128)(2,1)} %get-tuple-element.465) | copy-start | bytes 101380
  84.1 3.0 %copy-start = (bf16[2,256,384]{2,1,0:T(8,128)(2,1)}, bf16[2,256,384]{2,1,0:T(8,128)(2,1)S(1)}, u32[]{:S(2)}) copy-start(bf16[2,256,384]{2,1,0:T(8,128)(2,1)S(1)} %rev.15) | copy-start | bytes 1179652
  87.0 1.2 copy-start.2
  87.0 5.6 %copy-start.34 = (f32[12]{0:T(128)S(1)}, f32[12]{0:T(128)}, u32[]{:S(2)}) copy-start(f32[12]{0:T(128)} %get-tuple-element.489) | copy-start | bytes 148
  87.1 5.6 %copy-start.35 = (f32[12]{0:T(128)S(1)}, f32[12]{0:T(128)}, u32[]{:S(2)}) copy-start(f32[12]{0:T(128)} %get-tuple-element.492) | copy-start | bytes 148
  87.1 5.8 %copy-start.27 = (f32[32]{0:T(128)S(1)}, f32[32]{0:T(128)}, u32[]{:S(2)}) copy-start(f32[32]{0:T(128)} %get-tuple-element.475) | copy-start | bytes 388
  87.1 5.8 %copy-start.28 = (f32[32]{0:T(128)S(1)}, f32[32]{0:T(128)}, u32[]{:S(2)}) copy-start(f32[32]{0:T(128)} %get-tuple-element.479) | copy-start | bytes 388
  87.1 5.8 %copy-start.29 = (f32[32]{0:T(128)S(1)}, f32[32]{0:T(128)}, u32[]{:S(2)}) copy-start(f32[32]{0:T(128)} %get-tuple-element.481) | copy-start | bytes 388
  87.1 5.8 %copy-start.30 = (f32[32]{0:T(128)S(1)}, f32[32]{0:T(128)}, u32[]{:S(2)}) copy-start(f32[32]{0:T(128)} %get-tuple-element.482) | copy-start | bytes 388
  87.1 5.8 %copy-start.32 = (f32[32]{0:T(128)S(1)}, f32[32]{0:T(128)}, u32[]{:S(2)}) copy-start(f32[32]{0:T(128)} %get-tuple-element.483) | copy-start | bytes 388
  87.1 6.6 %copy-start.16 = (f32[768]{0:T(1024)S(1)}, f32[768]{0:T(1024)}, u32[]{:S(2)}) copy-start(f32[768]{0:T(1024)} %get-tuple-element.371) | copy-start | bytes 9220
  87.1 6.6 %copy-start.17 = (f32[768]{0:T(1024)S(1)}, f32[768]{0:T(1024)}, u32[]{:S(2)}) copy-start(f32[768]{0:T(1024)} %get-tuple-element.372) | copy-start | bytes 9220
  87.1 6.6 %copy-start.18 = (f32[768]{0:T(1024)S(1)}, f32[768]{0:T(1024)}, u32[]{:S(2)}) copy-start(f32[768]{0:T(1024)} %get-tuple-element.373) | copy-start | bytes 9220
  87.1 6.6 %copy-start.19 = (f32[768]{0:T(1024)S(1)}, f32[768]{0:T(1024)}, u32[]{:S(2)}) copy-start(f32[768]{0:T(1024)} %get-tuple-element.374) | copy-start | bytes 9220
  87.2 6.6 %copy-start.20 = (f32[768]{0:T(1024)S(1)}, f32[768]{0:T(1024)}, u32[]{:S(2)}) copy-start(f32[768]{0:T(1024)} %get-tuple-element.379) | copy-start | bytes 9220
  88.2 4.7 %collective-permute-start.3 = (bf16[3,32]{0,1:T(8,128)(2,1)S(1)}, bf16[3,32]{0,1:T(8,128)(2,1)S(1)}, u32[]{:S(2)}, u32[]{:S(2)}) collective-permute-start(bf16[3,32]{0,1:T(8,128)(2,1)S(1)} %slice.390), channel_id=1, source_target_pairs={{0,1},{1,2},{2,3},{3,4},{4,5},{5,6},{6,7},{8,9},{9,10},{10,11},{11... | collective-permute-start | bytes 584 | tf_op jit(solution)/shard_map/ppermute | solution.py:36
  89.5 4.2 %collective-permute-start.2 = (bf16[3,768]{1,0:T(4,128)(2,1)S(1)}, bf16[3,768]{1,0:T(4,128)(2,1)S(1)}, u32[]{:S(2)}, u32[]{:S(2)}) collective-permute-start(bf16[3,768]{1,0:T(4,128)(2,1)S(1)} %slice.384), channel_id=1, source_target_pairs={{0,1},{1,2},{2,3},{3,4},{4,5},{5,6},{6,7},{8,9},{9,10},{10,11},{11... | collective-permute-start | bytes 13832 | tf_op jit(solution)/shard_map/ppermute | solution.py:36
  96.2 0.6 copy-start.7
  98.0 2.1 %copy-start.8 = (f32[2,256,12]{1,0,2:T(2,128)S(1)}, f32[2,256,12]{1,0,2:T(2,128)}, u32[]{:S(2)}) copy-start(f32[2,256,12]{1,0,2:T(2,128)} %copy-done.7) | copy-start | bytes 73732 | tf_op jit(solution)/shard_map/while
  100.2 0.6 copy-start.7
  102.0 2.1 %copy-start.8 = (f32[2,256,12]{1,0,2:T(2,128)S(1)}, f32[2,256,12]{1,0,2:T(2,128)}, u32[]{:S(2)}) copy-start(f32[2,256,12]{1,0,2:T(2,128)} %copy-done.7) | copy-start | bytes 73732 | tf_op jit(solution)/shard_map/while
  106.3 24.7 %copy-start.13 = (bf16[2,256,16]{1,0,2:T(2,128)(2,1)S(1)}, bf16[2,256,16]{1,0,2:T(2,128)(2,1)}, u32[]{:S(2)}) copy-start(bf16[2,256,16]{1,0,2:T(2,128)(2,1)} %reshape.384) | copy-start | bytes 49156
  106.3 24.7 %copy-start.31 = (f32[12]{0:T(128)S(1)}, f32[12]{0:T(128)}, u32[]{:S(2)}) copy-start(f32[12]{0:T(128)} %get-tuple-element.485) | copy-start | bytes 148
  134.1 1.9 %copy-start.1 = (bf16[2,256,384]{2,1,0:T(8,128)(2,1)S(1)}, bf16[2,256,384]{2,1,0:T(8,128)(2,1)}, u32[]{:S(2)}) copy-start(bf16[2,256,384]{2,1,0:T(8,128)(2,1)} %copy-done) | copy-start | bytes 1179652
  134.1 1.9 %copy-start.3 = (bf16[512,1536]{1,0:T(8,128)(2,1)S(1)}, bf16[512,1536]{1,0:T(8,128)(2,1)}, u32[]{:S(2)}) copy-start(bf16[512,1536]{1,0:T(8,128)(2,1)} %copy-done.2) | copy-start | bytes 4718596
  134.1 1.9 %copy-start.24 = (f32[768]{0:T(1024)S(1)}, f32[768]{0:T(1024)}, u32[]{:S(2)}) copy-start(f32[768]{0:T(1024)} %get-tuple-element.381) | copy-start | bytes 9220
where the time goes:
time: 140 us; the launch traced here: 139 us
  blocking collectives  48.3 us (34%)
  local copies, waits for them, and re-layouts  28.6 us (20%)
  matrix products  17.9 us (13%)
  starting transfers between devices  17.7 us (13%)
  other arithmetic  13.7 us (10%)
  waiting for transfers between devices  9.95 us (7%)
  between operations  1.55 us (1%)
    unnamed x2, blocking collectives  26.5 us
    all_gather x2, blocking collectives, entering_2(): lax.all_gather(a.astype(kind), axis)  21.8 us
    ppermute x4, starting transfers between devices, passed_along(): lax.ppermute(value, axis, [(source, source + steps) for source in range(f...  8.94 us
    all_to_all x1, waiting for transfers between devices, on_device(): lax.all_to_all(row_grid, 'seq', split_axis=0, concat_axis=1, tiled=True)  8.22 us
    all_to_all x1, starting transfers between devices, on_device(): lax.all_to_all(flipped, 'seq', split_axis=1, concat_axis=0, tiled=True)  5.2 us
    dot_general x2, matrix products, mixer(): jnp.dot(normed, in_weight[layer], preferred_element_type=jnp.float32)  4.51 us
    unnamed x80, local copies, waits for them, and re-layouts  4.07 us
    reduce_sum x4, other arithmetic, rms_scaled(): jnp.mean(values * values, axis=-1, keepdims=True) + epsilon  3.99 us
  transfers between devices with their start and end apart: 6, of which 2 were waited for; matrix products, arithmetic and copies ran while one was open for 6% of the time, Pallas kernels for 0%

commit v1 on v0

--- a/solution.py
+++ b/solution.py
@@ -188,7 +188,10 @@
     row_grid = jnp.transpose(layer_out.reshape(block_cols, full_rows, feature_count), (1, 0, 2))[
         ::-1
     ]
-    returned = lax.all_to_all(row_grid, "seq", split_axis=0, concat_axis=1, tiled=True)
+    returned = jnp.concatenate(
+        lax.all_to_all(jnp.stack(jnp.split(row_grid, lax.axis_size("seq"), axis=0)), "seq", 0, 0),
+        axis=1,
+    )
     second = returned[:, ::-1, :].reshape(row_count * col_count, feature_count)
     mixed_out = mixer(second, 1, *params)
     result = (

time: 140 us -> 148 us (1.057)
  local copies, waits for them, and re-layouts: 28.6 us -> 37.7 us
    unnamed x80 -> x87, local copies, waits for them, and re-layouts: 4.07 us -> 8.64 us
    dynamic_slice x12, local copies, waits for them, and re-layouts: 0.13 us -> 3.07 us  [mixer(): intra_out, local_states, cumulative = lax.map(group_terms, inputs)]
    split x0 -> x9, local copies, waits for them, and re-layouts: none -> 2.9 us  [on_device(): jnp.split(row_grid, lax.axis_size('seq'), axis=0)]
    while x24 -> x8, local copies, waits for them, and re-layouts: 2.31 us -> 0.05 us
where the time goes in v1:
time: 148 us; the launch traced here: 146 us
  blocking collectives  47.3 us (32%)
  local copies, waits for them, and re-layouts  37.7 us (25%)
  matrix products  17.9 us (12%)
  starting transfers between devices  17.6 us (12%)
  other arithmetic  13.7 us (9%)
  waiting for transfers between devices  10 us (7%)
  between operations  1.55 us (1%)
    unnamed x2, blocking collectives  26.7 us
    all_gather x2, blocking collectives, entering_2(): lax.all_gather(a.astype(kind), axis)  20.6 us
    ppermute x4, starting transfers between devices, passed_along(): lax.ppermute(value, axis, [(source, source + steps) for source in range(f...  8.95 us
    unnamed x87, local copies, waits for them, and re-layouts  8.64 us
    all_to_all x1, waiting for transfers between devices, on_device(): lax.all_to_all(jnp.stack(jnp.split(row_grid, lax.axis_size('seq'), axis=0...  8.22 us
    all_to_all x1, starting transfers between devices, on_device(): lax.all_to_all(flipped, 'seq', split_axis=1, concat_axis=0, tiled=True)  5.2 us
    dot_general x2, matrix products, mixer(): jnp.dot(normed, in_weight[layer], preferred_element_type=jnp.float32)  4.49 us
    reduce_sum x4, other arithmetic, rms_scaled(): jnp.mean(values * values, axis=-1, keepdims=True) + epsilon  3.99 us
  transfers between devices with their start and end apart: 6, of which 2 were waited for; matrix products, arithmetic and copies ran while one was open for 6% of the time, Pallas kernels for 0%

profile of v1, /device:TPU:0, one launch (start us, length us, event | category | flops | bytes accessed | tf_op | source)
XLA Modules:
  0.0 146.5 jit_solution(9471441603950000450)
XLA Ops:
  0.1 1.5 %copy.98 = bf16[2,256,384]{2,0,1:T(2,128)(2,1)S(1)} copy(bf16[2,256,384]{2,1,0:T(8,128)(2,1)} %param.23) | data formatting | bytes 786432 | tf_op args[0]
  1.5 1.0 rev.10
  2.5 5.2 %all-to-all-start = ((bf16[2,256,384]{2,0,1:T(2,128)(2,1)}), bf16[2,256,384]{2,0,1:T(2,128)(2,1)S(1)}, u32[]{:S(2)}, u32[]{:S(2)}) async-start(bf16[2,256,384]{2,0,1:T(2,128)(2,1)} %rev.10), calls=%async_computation | async-start | bytes 786432 | tf_op jit(solution)/shard_map/all_to_all | solution.py:178
  8.3 0.6 slice_reduce_fusion.13
  8.9 0.6 slice_reduce_fusion.20
  10.6 0.6 slice_reduce_fusion.8
  12.9 0.6 slice_reduce_fusion.12
  13.6 0.7 fusion.106
  14.3 1.8 %all-to-all-done = bf16[2,256,384]{2,0,1:T(2,128)(2,1)S(1)} async-done(((bf16[2,256,384]{2,0,1:T(2,128)(2,1)}), bf16[2,256,384]{2,0,1:T(2,128)(2,1)S(1)}, u32[]{:S(2)}, u32[]{:S(2)}) %all-to-all-start) | async-done | bytes 393248 | tf_op jit(solution)/shard_map/all_to_all | solution.py:178
  17.5 2.2 %convolution_convert_fusion.1 = bf16[512,1536]{1,0:T(8,128)(2,1)S(1)} fusion(bf16[512,384]{1,0:T(8,128)(2,1)S(1)} %bitcast.360, bf16[2,384,1536]{2,1,0:T(8,128)(2,1)} %param.25), kind=kOutput, calls=%fused_computation.95 | convolution fusion | flops 604766208 | bytes 3145728 | tf_op jit(solution)/shard_map/dot_general | solution.py:94
  19.8 1.0 convert_element_type.292
  21.1 1.3 collective-permute-start.1
  22.4 3.2 %collective-permute-start = (bf16[3,768]{1,0:T(4,128)(2,1)S(1)}, bf16[3,768]{1,0:T(4,128)(2,1)S(1)}, u32[]{:S(2)}, u32[]{:S(2)}) collective-permute-start(bf16[3,768]{1,0:T(4,128)(2,1)S(1)} %slice.376), channel_id=1, source_target_pairs={{0,1},{1,2},{2,3},{3,4},{4,5},{5,6},{6,7},{8,9},{9,10},{10,11},{11... | collective-permute-start | bytes 13832 | tf_op jit(solution)/shard_map/ppermute | solution.py:36
  25.8 0.6 reshape.386
  26.6 0.6 reshape.383
  27.2 1.1 multiply_convert_fusion.17
  29.0 0.6 broadcast.140.clone
  29.7 8.3 %while.78 = (s32[]{:T(128)}, f32[2,256,12,64]{1,3,2,0:T(8,128)S(1)}, f32[2,12,64,16]{2,3,1,0:T(8,128)S(1)}, f32[2,256,12]{1,2,0:T(8,128)}, bf16[2,256,12,64]{1,3...) while((s32[]{:T(128)}, ...), condition=%wide.region_4.5_spmd, body=%wide.region_1.4_spmd.sunk | while | flops 114038824 | bytes 2769885 | solution.py:132
  29.7 0.8 constant_dynamic-slice_fusion.8
  31.6 1.0 fusion.139
  33.2 0.6 bitcast_dynamic-update-slice_fusion.16
  33.8 0.8 constant_dynamic-slice_fusion.8
  35.8 1.0 fusion.139
  37.3 0.6 bitcast_dynamic-update-slice_fusion.16
  37.9 1.0 slice_reduce_fusion.6
  38.9 0.8 exp.113
  40.1 10.3 %all-gather.1 = bf16[96,64,16]{1,2,0:T(8,128)(2,1)S(1)} all-gather(bf16[12,64,16]{1,2,0:T(8,128)(2,1)S(1)} %convert_element_type.257), channel_id=3, replica_groups=mesh['dp'=4,'seq'=8] {'seq'}, dimensions={0}, use_global_device_ids=true | all-gather | bytes 221184 | tf_op jit(solution)/shard_map/all_gather | solution.py:16
  50.6 13.2 %all-reduce = bf16[96]{0:T(256)(128)(2,1)S(1)} all-reduce(bf16[96]{0:T(256)(128)(2,1)S(1)} %dynamic-update-slice), channel_id=2, replica_groups=mesh['dp'=4,'seq'=8] {'seq'}, use_global_device_ids=true, to_apply=%add | all-reduce | flops 96 | bytes 384
  64.2 1.3 multiply_add_fusion.1
  65.5 1.2 copy.109
  67.4 1.9 %multiply_reduce_fusion.1 = f32[512]{0:T(512)S(1)} fusion(f32[512,768]{1,0:T(8,128)S(1)} %copy.110, bf16[512,1536]{1,0:T(8,128)(2,1)} %copy-done.4), kind=kLoop, calls=%fused_computation.113 | loop fusion | flops 3145216 | bytes 2361344 | tf_op jit(solution)/shard_map/reduce_sum | solution.py:42
  69.3 1.9 %fusion.68 = bf16[512,384]{1,0:T(8,128)(2,1)S(1)} fusion(f32[512,384]{1,0:T(8,128)S(1)} %bitcast.363, f32[768]{0:T(1024)S(1)} %copy-done.21, f32[512]{0:T(512)S(1)} %add_rsqrt_fusion.3, bf16[2,768,384]{2,1,0:T(8,128)(2,1)} %param.33, f32[512,768]{1,0:T(8,128)S(1)} %copy.110, bf16[512,1536]{1,0:T(8,128)(2,1)S(1)} %copy-done.5), kind=kOutput, calls=%fused_computation.118 | convolution fusion | flops 305922048 | bytes 4134912 | tf_op jit(solution)/shard_map/dot_general | solution.py:186
  71.7 0.7 bitcast_dynamic-update-slice_fusion.11
  74.7 0.7 bitcast_dynamic-update-slice_fusion.10
  75.4 0.7 bitcast_dynamic-update-slice_fusion.9
  76.1 0.7 bitcast_dynamic-update-slice_fusion.8
  76.7 0.7 bitcast_dynamic-update-slice_fusion.7
  77.4 0.7 bitcast_dynamic-update-slice_fusion.6
  78.0 0.7 bitcast_dynamic-update-slice_fusion.5
  78.7 0.7 bitcast_dynamic-update-slice_fusion.4
  79.3 3.5 %all-to-all-start.1 = ((bf16[8,2,32,384]{3,1,2,0:T(2,128)(2,1)}), bf16[8,2,32,384]{3,1,2,0:T(2,128)(2,1)S(1)}, u32[]{:S(2)}, u32[]{:S(2)}) async-start(bf16[8,2,32,384]{3,1,2,0:T(2,128)(2,1)} %bitcast_dynamic-update-slice_fusion.4), calls=%async_computation.1 | async-start | bytes 786432 | tf_op jit(solution)/shard_map/all_to_all | solution.py:192
  82.8 8.2 %all-to-all-done.1 = bf16[8,2,32,384]{3,1,2,0:T(2,128)(2,1)S(1)} async-done(((bf16[8,2,32,384]{3,1,2,0:T(2,128)(2,1)}), bf16[8,2,32,384]{3,1,2,0:T(2,128)(2,1)S(1)}, u32[]{:S(2)}, u32[]{:S(2)}) %all-to-all-start.1) | async-done | bytes 393248 | tf_op jit(solution)/shard_map/all_to_all | solution.py:192
  92.3 2.2 %convolution_convert_fusion = bf16[512,1536]{1,0:T(8,128)(2,1)S(1)} fusion(bf16[512,384]{1,0:T(8,128)(2,1)S(1)} %bitcast.358, bf16[2,384,1536]{2,1,0:T(8,128)(2,1)} %param.25), kind=kOutput, calls=%fused_computation.94 | convolution fusion | flops 604766208 | bytes 3145728 | tf_op jit(solution)/shard_map/dot_general | solution.py:94
  94.7 1.0 copy-done.2
  95.7 1.3 collective-permute-start.3
  97.0 3.2 %collective-permute-start.2 = (bf16[3,768]{1,0:T(4,128)(2,1)S(1)}, bf16[3,768]{1,0:T(4,128)(2,1)S(1)}, u32[]{:S(2)}, u32[]{:S(2)}) collective-permute-start(bf16[3,768]{1,0:T(4,128)(2,1)S(1)} %slice.392), channel_id=1, source_target_pairs={{0,1},{1,2},{2,3},{3,4},{4,5},{5,6},{6,7},{8,9},{9,10},{10,11},{11... | collective-permute-start | bytes 13832 | tf_op jit(solution)/shard_map/ppermute | solution.py:36
  100.3 0.6 reshape.395
  101.2 0.6 reshape.392
  101.8 1.1 multiply_convert_fusion.15
  104.3 8.3 %while.80 = (s32[]{:T(128)}, f32[2,256,12,64]{1,3,2,0:T(8,128)S(1)}, f32[2,12,64,16]{2,3,1,0:T(8,128)S(1)}, f32[2,256,12]{1,2,0:T(8,128)}, bf16[2,256,12,64]{1,3...) while((s32[]{:T(128)}, ...), condition=%wide.region_16.17_spmd, body=%wide.region_13.16_spmd.sunk | while | flops 114038824 | bytes 2769885 | solution.py:132
  104.3 0.8 constant_dynamic-slice_fusion.9
  106.3 1.0 fusion.148
  107.8 0.6 bitcast_dynamic-update-slice_fusion.17
  108.4 0.8 constant_dynamic-slice_fusion.9
  110.4 1.0 fusion.148
  112.0 0.6 bitcast_dynamic-update-slice_fusion.17
  112.6 1.0 slice_reduce_fusion.4
  113.5 0.8 exp.120
  114.7 10.3 %all-gather.3 = bf16[96,64,16]{1,2,0:T(8,128)(2,1)S(1)} all-gather(bf16[12,64,16]{1,2,0:T(8,128)(2,1)S(1)} %convert_element_type.282), channel_id=5, replica_groups=mesh['dp'=4,'seq'=8] {'seq'}, dimensions={0}, use_global_device_ids=true | all-gather | bytes 221184 | tf_op jit(solution)/shard_map/all_gather | solution.py:16
  125.2 13.5 %all-reduce.1 = bf16[96]{0:T(256)(128)(2,1)S(1)} all-reduce(bf16[96]{0:T(256)(128)(2,1)S(1)} %dynamic-update-slice.1), channel_id=4, replica_groups=mesh['dp'=4,'seq'=8] {'seq'}, use_global_device_ids=true, to_apply=%add.1 | all-reduce | flops 96 | bytes 384
  138.8 1.3 multiply_add_fusion
  140.1 1.2 copy.121
  142.0 1.8 %multiply_reduce_fusion = f32[512]{0:T(512)S(1)} fusion(f32[512,768]{1,0:T(8,128)S(1)} %copy.122, bf16[512,1536]{1,0:T(8,128)(2,1)} %copy-done.2), kind=kLoop, calls=%fused_computation.109 | loop fusion | flops 3145216 | bytes 2361344 | tf_op jit(solution)/shard_map/reduce_sum | solution.py:42
  143.9 2.6 %fusion.69 = bf16[512,384]{1,0:T(8,128)(2,1)} fusion(f32[768]{0:T(1024)S(1)} %copy-done.20, f32[512]{0:T(512)S(1)} %add_rsqrt_fusion.1, bf16[2,768,384]{2,1,0:T(8,128)(2,1)} %param.33, f32[512,768]{1,0:T(8,128)S(1)} %copy.122, bf16[512,1536]{1,0:T(8,128)(2,1)S(1)} %copy-done.3, bf16[512,384]{1,0:T(8,128)(2,1)S(1)} %bitcast.350), kind=kOutput, calls=%fused_computation.119 | convolution fusion | flops 306118656 | bytes 3741696 | tf_op jit(solution)/shard_map/dot_general | solution.py:199
  (240 shorter events, 21.4 us)
Async XLA Ops:
  0.0 11.8 %copy-start.35 = (u32[32]{0:T(128)S(1)}, u32[32]{0:T(128)}, u32[]{:S(2)}) copy-start(u32[32]{0:T(128)} %constant.128) | copy-start | bytes 388
  0.0 7.7 %copy-start.18 = (f32[2,800]{1,0:T(2,128)S(1)}, f32[2,800]{1,0:T(2,128)}, u32[]{:S(2)}) copy-start(f32[2,800]{1,0:T(2,128)} %param.28) | copy-start | bytes 19204
  0.0 8.9 %copy-start.22 = (f32[2,384]{1,0:T(2,128)S(1)}, f32[2,384]{1,0:T(2,128)}, u32[]{:S(2)}) copy-start(f32[2,384]{1,0:T(2,128)} %param.24) | copy-start | bytes 9220
  0.0 9.5 %copy-start.11 = (f32[2,4,800]{2,1,0:T(4,128)S(1)}, f32[2,4,800]{2,1,0:T(4,128)}, u32[]{:S(2)}) copy-start(f32[2,4,800]{2,1,0:T(4,128)} %param.27) | copy-start | bytes 76804
  0.0 10.1 %copy-start.32 = (f32[2,12]{1,0:T(2,128)S(1)}, f32[2,12]{1,0:T(2,128)}, u32[]{:S(2)}) copy-start(f32[2,12]{1,0:T(2,128)} %param.31) | copy-start | bytes 292
  0.0 10.6 %copy-start.19 = (f32[2,768]{1,0:T(2,128)S(1)}, f32[2,768]{1,0:T(2,128)}, u32[]{:S(2)}) copy-start(f32[2,768]{1,0:T(2,128)} %param.32) | copy-start | bytes 18436
  0.0 11.2 %copy-start.34 = (f32[2,12]{1,0:T(2,128)S(1)}, f32[2,12]{1,0:T(2,128)}, u32[]{:S(2)}) copy-start(f32[2,12]{1,0:T(2,128)} %param.29) | copy-start | bytes 292
  0.0 11.2 %copy-start.33 = (f32[2,12]{1,0:T(2,128)S(1)}, f32[2,12]{1,0:T(2,128)}, u32[]{:S(2)}) copy-start(f32[2,12]{1,0:T(2,128)} %param.30) | copy-start | bytes 292
  0.0 13.5 %copy-start.7 = (bf16[2,384,44]{1,0,2:T(2,128)(2,1)S(1)}, bf16[2,384,44]{1,0,2:T(2,128)(2,1)}, u32[]{:S(2)}) copy-start(bf16[2,384,44]{1,0,2:T(2,128)(2,1)} %param.26) | copy-start | bytes 202756
  2.5 13.5 %all-to-all-start = ((bf16[2,256,384]{2,0,1:T(2,128)(2,1)}), bf16[2,256,384]{2,0,1:T(2,128)(2,1)S(1)}, u32[]{:S(2)}, u32[]{:S(2)}) async-start(bf16[2,256,384]{2,0,1:T(2,128)(2,1)} %rev.10), calls=%async_computation | async-start | bytes 786432 | tf_op jit(solution)/shard_map/all_to_all | solution.py:178
  19.7 1.4 copy-start.4
  21.1 5.3 %collective-permute-start.1 = (bf16[3,32]{0,1:T(8,128)(2,1)S(1)}, bf16[3,32]{0,1:T(8,128)(2,1)S(1)}, u32[]{:S(2)}, u32[]{:S(2)}) collective-permute-start(bf16[3,32]{0,1:T(8,128)(2,1)S(1)} %slice.382), channel_id=1, source_target_pairs={{0,1},{1,2},{2,3},{3,4},{4,5},{5,6},{6,7},{8,9},{9,10},{10,11},{11... | collective-permute-start | bytes 584 | tf_op jit(solution)/shard_map/ppermute | solution.py:36
  22.4 4.8 %collective-permute-start = (bf16[3,768]{1,0:T(4,128)(2,1)S(1)}, bf16[3,768]{1,0:T(4,128)(2,1)S(1)}, u32[]{:S(2)}, u32[]{:S(2)}) collective-permute-start(bf16[3,768]{1,0:T(4,128)(2,1)S(1)} %slice.376), channel_id=1, source_target_pairs={{0,1},{1,2},{2,3},{3,4},{4,5},{5,6},{6,7},{8,9},{9,10},{10,11},{11... | collective-permute-start | bytes 13832 | tf_op jit(solution)/shard_map/ppermute | solution.py:36
  40.1 24.1 %copy-start.10 = (bf16[2,256,16]{1,0,2:T(2,128)(2,1)S(1)}, bf16[2,256,16]{1,0,2:T(2,128)(2,1)}, u32[]{:S(2)}) copy-start(bf16[2,256,16]{1,0,2:T(2,128)(2,1)} %reshape.383) | copy-start | bytes 49156
  40.1 24.1 %copy-start.29 = (f32[12]{0:T(128)S(1)}, f32[12]{0:T(128)}, u32[]{:S(2)}) copy-start(f32[12]{0:T(128)} %get-tuple-element.494) | copy-start | bytes 148
  67.3 1.9 %copy-start.5 = (bf16[512,1536]{1,0:T(8,128)(2,1)S(1)}, bf16[512,1536]{1,0:T(8,128)(2,1)}, u32[]{:S(2)}) copy-start(bf16[512,1536]{1,0:T(8,128)(2,1)} %copy-done.4) | copy-start | bytes 4718596
  67.3 1.9 %copy-start.6 = (f32[16,32,384]{2,0,1:T(8,128)S(1)}, f32[16,32,384]{2,0,1:T(8,128)}, u32[]{:S(2)}) copy-start(f32[16,32,384]{2,0,1:T(8,128)} %convert_element_type.292) | copy-start | bytes 2359300
  67.4 1.9 %copy-start.21 = (f32[768]{0:T(1024)S(1)}, f32[768]{0:T(1024)}, u32[]{:S(2)}) copy-start(f32[768]{0:T(1024)} %get-tuple-element.382) | copy-start | bytes 9220
  76.7 15.1 %copy-start.17 = (f32[384]{0:T(512)S(1)}, f32[384]{0:T(512)}, u32[]{:S(2)}) copy-start(f32[384]{0:T(512)} %get-tuple-element.383) | copy-start | bytes 4612
  79.3 11.7 %all-to-all-start.1 = ((bf16[8,2,32,384]{3,1,2,0:T(2,128)(2,1)}), bf16[8,2,32,384]{3,1,2,0:T(2,128)(2,1)S(1)}, u32[]{:S(2)}, u32[]{:S(2)}) async-start(bf16[8,2,32,384]{3,1,2,0:T(2,128)(2,1)} %bitcast_dynamic-update-slice_fusion.4), calls=%async_computation.1 | async-start | bytes 786432 | tf_op jit(solution)/shard_map/all_to_all | solution.py:192
  82.8 9.2 %copy-start.8 = (bf16[1,384,44]{1,0,2:T(2,128)(2,1)S(1)}, bf16[1,384,44]{1,0,2:T(2,128)(2,1)}, u32[]{:S(2)}) copy-start(bf16[1,384,44]{1,0,2:T(2,128)(2,1)} %get-tuple-element.473) | copy-start | bytes 101380
  91.6 3.0 %copy-start = (bf16[2,256,384]{2,1,0:T(8,128)(2,1)}, bf16[2,256,384]{2,1,0:T(8,128)(2,1)S(1)}, u32[]{:S(2)}) copy-start(bf16[2,256,384]{2,1,0:T(8,128)(2,1)S(1)} %rev.12) | copy-start | bytes 1179652
  94.6 1.2 copy-start.2
  94.6 5.6 %copy-start.30 = (f32[12]{0:T(128)S(1)}, f32[12]{0:T(128)}, u32[]{:S(2)}) copy-start(f32[12]{0:T(128)} %get-tuple-element.497) | copy-start | bytes 148
  94.6 5.6 %copy-start.31 = (f32[12]{0:T(128)S(1)}, f32[12]{0:T(128)}, u32[]{:S(2)}) copy-start(f32[12]{0:T(128)} %get-tuple-element.500) | copy-start | bytes 148
  94.6 6.4 %copy-start.23 = (f32[32]{0:T(128)S(1)}, f32[32]{0:T(128)}, u32[]{:S(2)}) copy-start(f32[32]{0:T(128)} %get-tuple-element.483) | copy-start | bytes 388
  94.6 6.4 %copy-start.24 = (f32[32]{0:T(128)S(1)}, f32[32]{0:T(128)}, u32[]{:S(2)}) copy-start(f32[32]{0:T(128)} %get-tuple-element.487) | copy-start | bytes 388
  94.6 6.4 %copy-start.25 = (f32[32]{0:T(128)S(1)}, f32[32]{0:T(128)}, u32[]{:S(2)}) copy-start(f32[32]{0:T(128)} %get-tuple-element.489) | copy-start | bytes 388
  94.6 6.4 %copy-start.26 = (f32[32]{0:T(128)S(1)}, f32[32]{0:T(128)}, u32[]{:S(2)}) copy-start(f32[32]{0:T(128)} %get-tuple-element.490) | copy-start | bytes 388
  94.6 6.4 %copy-start.28 = (f32[32]{0:T(128)S(1)}, f32[32]{0:T(128)}, u32[]{:S(2)}) copy-start(f32[32]{0:T(128)} %get-tuple-element.491) | copy-start | bytes 388
  94.6 7.2 %copy-start.12 = (f32[768]{0:T(1024)S(1)}, f32[768]{0:T(1024)}, u32[]{:S(2)}) copy-start(f32[768]{0:T(1024)} %get-tuple-element.371) | copy-start | bytes 9220
  94.6 7.2 %copy-start.13 = (f32[768]{0:T(1024)S(1)}, f32[768]{0:T(1024)}, u32[]{:S(2)}) copy-start(f32[768]{0:T(1024)} %get-tuple-element.372) | copy-start | bytes 9220
  94.7 7.2 %copy-start.14 = (f32[768]{0:T(1024)S(1)}, f32[768]{0:T(1024)}, u32[]{:S(2)}) copy-start(f32[768]{0:T(1024)} %get-tuple-element.373) | copy-start | bytes 9220
  94.7 7.2 %copy-start.15 = (f32[768]{0:T(1024)S(1)}, f32[768]{0:T(1024)}, u32[]{:S(2)}) copy-start(f32[768]{0:T(1024)} %get-tuple-element.374) | copy-start | bytes 9220
  94.7 7.2 %copy-start.16 = (f32[768]{0:T(1024)S(1)}, f32[768]{0:T(1024)}, u32[]{:S(2)}) copy-start(f32[768]{0:T(1024)} %get-tuple-element.379) | copy-start | bytes 9220
  95.7 5.2 %collective-permute-start.3 = (bf16[3,32]{0,1:T(8,128)(2,1)S(1)}, bf16[3,32]{0,1:T(8,128)(2,1)S(1)}, u32[]{:S(2)}, u32[]{:S(2)}) collective-permute-start(bf16[3,32]{0,1:T(8,128)(2,1)S(1)} %slice.398), channel_id=1, source_target_pairs={{0,1},{1,2},{2,3},{3,4},{4,5},{5,6},{6,7},{8,9},{9,10},{10,11},{11... | collective-permute-start | bytes 584 | tf_op jit(solution)/shard_map/ppermute | solution.py:36
  97.0 4.8 %collective-permute-start.2 = (bf16[3,768]{1,0:T(4,128)(2,1)S(1)}, bf16[3,768]{1,0:T(4,128)(2,1)S(1)}, u32[]{:S(2)}, u32[]{:S(2)}) collective-permute-start(bf16[3,768]{1,0:T(4,128)(2,1)S(1)} %slice.392), channel_id=1, source_target_pairs={{0,1},{1,2},{2,3},{3,4},{4,5},{5,6},{6,7},{8,9},{9,10},{10,11},{11... | collective-permute-start | bytes 13832 | tf_op jit(solution)/shard_map/ppermute | solution.py:36
  114.7 24.1 %copy-start.9 = (bf16[2,256,16]{1,0,2:T(2,128)(2,1)S(1)}, bf16[2,256,16]{1,0,2:T(2,128)(2,1)}, u32[]{:S(2)}) copy-start(bf16[2,256,16]{1,0,2:T(2,128)(2,1)} %reshape.392) | copy-start | bytes 49156
  114.7 24.1 %copy-start.27 = (f32[12]{0:T(128)S(1)}, f32[12]{0:T(128)}, u32[]{:S(2)}) copy-start(f32[12]{0:T(128)} %get-tuple-element.493) | copy-start | bytes 148
  142.0 1.9 %copy-start.1 = (bf16[2,256,384]{2,1,0:T(8,128)(2,1)S(1)}, bf16[2,256,384]{2,1,0:T(8,128)(2,1)}, u32[]{:S(2)}) copy-start(bf16[2,256,384]{2,1,0:T(8,128)(2,1)} %copy-done) | copy-start | bytes 1179652
  142.0 1.9 %copy-start.3 = (bf16[512,1536]{1,0:T(8,128)(2,1)S(1)}, bf16[512,1536]{1,0:T(8,128)(2,1)}, u32[]{:S(2)}) copy-start(bf16[512,1536]{1,0:T(8,128)(2,1)} %copy-done.2) | copy-start | bytes 4718596
  142.0 1.9 %copy-start.20 = (f32[768]{0:T(1024)S(1)}, f32[768]{0:T(1024)}, u32[]{:S(2)}) copy-start(f32[768]{0:T(1024)} %get-tuple-element.381) | copy-start | bytes 9220
